TPU v7x, 512 devices: a whole 4x4x16 slice. The times are simulated.
512 devices in a mesh: pos: 16 (over z_lo, x), slab: 32 (over z_hi, y, core).
Axes of the slice: x: 4, y: 4, z: 16 (z_hi: 4, z_lo: 4; z = z_hi * 4 + z_lo), core: 2. Of those that a mesh axis runs over, the one named last changes fastest.
Arguments:
- labels: int32 [64, 256, 256], P('slab'), may hold values from 0 to 3
- magnet_mask: int32 [64, 256, 256], P('slab'), may hold values 0 or 1
- reluctivity: float32 [4], replicated, may hold values from 0.3 to 3
- rotor_shift: int32 [16], P('pos'), may hold values from 0 to 255
- potential: float32 [16, 64, 256, 256], P('pos', 'slab'), may hold values from -6 to 6
- adjoint_load: float32 [16, 64, 256, 256], P('pos', 'slab'), may hold values from -40 to 40
Outputs:
- shape_gradient: float32 [64, 256, 256], P('slab')
- adjoint: float32 [16, 64, 256, 256], P('pos', 'slab')
All inputs are finite; a program needn't handle non-finite values. No bound on the sum of `magnet_mask` on one device may be relied on, other than what follows from the above.
Results may differ from a plain program's by a relative error of at most 0.0003.
Values sent between devices are 32-bit elements; how exact they have to be, the bound alone decides.
A program may use at most 64 MiB of HBM per device.

v0:
```python
import jax
import jax.numpy as jnp
from jax import lax
from jax.sharding import PartitionSpec as P

ITERS = 2
diagonal_shift = 0.5


def padded(shard, sides, width):
    for axis, dim in sides:
        size, length = (lax.axis_size(axis), shard.shape[dim])
        up = [(i, (i + 1) % size) for i in range(size - 1)]
        down = [(j, i) for i, j in up]
        last = lax.slice_in_dim(shard, length - width, length, axis=dim)
        first = lax.slice_in_dim(shard, 0, width, axis=dim)
        before = lax.ppermute(last, axis, up)
        after = lax.ppermute(first, axis, down)
        shard = jnp.concatenate([before, shard, after], axis=dim)
    return shard


def material_field(labels, reluctivity, offset):
    rotated = jnp.roll(labels, offset, axis=2)
    radial = lax.broadcasted_iota(jnp.int32, labels.shape, 1)
    material = jnp.where(radial < labels.shape[1] // 2, rotated, labels)
    result = jnp.zeros(labels.shape, jnp.float32)
    for index in range(4):
        result = result + (material == index).astype(jnp.float32) * reluctivity[index]
    return result


def apply_operator(field, padded_field, relief, padded_relief):
    result = diagonal_shift * field
    result = result + 0.5 * (relief + padded_relief[2:]) * (field - padded_field[2:])
    result = result + 0.5 * (relief + padded_relief[:-2]) * (field - padded_field[:-2])
    radial_field = jnp.pad(field, ((0, 0), (1, 1), (0, 0)))
    radial_relief = jnp.pad(relief, ((0, 0), (1, 1), (0, 0)))
    result = result + 0.5 * (relief + radial_relief[:, 2:]) * (field - radial_field[:, 2:])
    result = result + 0.5 * (relief + radial_relief[:, :-2]) * (field - radial_field[:, :-2])
    for offset in (1, -1):
        result = result + 0.5 * (relief + jnp.roll(relief, offset, 2)) * (
            field - jnp.roll(field, offset, 2)
        )
    return result


def gradient_term(stacked, padded_stack, relief, magnet_mask):
    axial = 0.5 * (padded_stack[:, 2:] - padded_stack[:, :-2])
    radial_pad = jnp.pad(stacked, ((0, 0), (0, 0), (1, 1), (0, 0)))
    radial = 0.5 * (radial_pad[:, :, 2:] - radial_pad[:, :, :-2])
    angular = 0.5 * (jnp.roll(stacked, -1, 3) - jnp.roll(stacked, 1, 3))
    inner = axial[0] * axial[1] + radial[0] * radial[1] + angular[0] * angular[1]
    square = axial[0] * axial[0] + radial[0] * radial[0] + angular[0] * angular[0]
    return magnet_mask.astype(jnp.float32) * relief * (inner + 0.5 * square)


def squares(residual):
    return lax.psum(jnp.sum(residual * residual), "slab")


def local(labels, magnet_mask, reluctivity, rotor_shift, potential, adjoint_load):
    relief = material_field(labels, reluctivity, rotor_shift[0])
    padded_relief = padded(relief, (("slab", 0),), 1)
    solution = jnp.zeros(relief.shape, jnp.float32)
    residual = adjoint_load[0]
    direction = residual
    norm_now = squares(residual)
    for iteration in range(ITERS):
        padded_field = padded(direction, (("slab", 0),), 1)
        image = apply_operator(direction, padded_field, relief, padded_relief)
        alpha = norm_now / lax.psum(jnp.sum(direction * image), "slab")
        solution = solution + alpha * direction
        residual = residual - alpha * image
        norm_next = squares(residual)
        direction = residual + norm_next / norm_now * direction
        norm_now = norm_next
    stacked = jnp.stack([potential[0], solution])
    padded_stack = padded(stacked, (("slab", 1),), 1)
    contribution = gradient_term(stacked, padded_stack, relief, magnet_mask)
    summed = lax.psum(contribution, "pos")
    return (summed / lax.axis_size("pos"), solution[None])


def solution(mesh):
    return jax.shard_map(
        local,
        mesh=mesh,
        in_specs=(
            P("slab", None, None),
            P("slab", None, None),
            P(),
            P("pos"),
            P("pos", "slab", None, None),
            P("pos", "slab", None, None),
        ),
        out_specs=(P("slab", None, None), P("pos", "slab", None, None)),
        check_vma=False,
    )
```

profile of v0, /device:TPU:8, one launch (start us, length us, event | category | flops | bytes accessed | tf_op | source)
XLA Modules:
  0.0 558.1 jit_solution(6151440687633539958)
XLA Ops:
  7.2 1.1 slice_bitcast_fusion.1
  8.3 1.9 collective-permute-start.3
  11.7 3.0 select_add_fusion
  14.7 3.6 collective-permute-start.2
  18.3 2.0 collective-permute-start.1
  20.3 5.6 %collective-permute-start = (f32[1,256,256]{2,1,0:T(8,128)S(1)}, f32[1,256,256]{2,1,0:T(8,128)S(1)}, u32[]{:S(2)}, u32[]{:S(2)}) collective-permute-start(f32[1,256,256]{2,1,0:T(8,128)S(1)} %get-tuple-element.21), channel_id=1, source_target_pairs={{1,0},{2,1},{3,2},{4,3},{5,4},{6,5},{7,6},{8,7},{9,8},{10,9},{11,1... | collective-permute-start | bytes 786440 | tf_op jit(solution)/shard_map/ppermute | solution.py:18
  26.5 3.3 collective-permute-done
  29.7 2.6 multiply_reduce_fusion.1
  32.3 91.9 %all-reduce.4 = (f32[]{:T(128)}, f32[]{:T(128)}) all-reduce(f32[]{:T(128)} %get-tuple-element.3, f32[]{:T(128)} %get-tuple-element.2), channel_id=1, replica_groups=mesh['pos'=16,'slab'=32] {'slab'}, use_global_device_ids=true, to_apply=%region_1.2 | all-reduce | flops 2 | bytes 16 | tf_op jit(solution)/shard_map/psum | solution.py:59
  125.6 0.7 multiply_reduce_fusion
  126.3 90.4 %psum.37 = f32[]{:T(128)} all-reduce(f32[]{:T(128)} %multiply_reduce_fusion), channel_id=1, replica_groups=mesh['pos'=16,'slab'=32] {'slab'}, use_global_device_ids=true, to_apply=%region_5.6 | all-reduce | flops 1 | bytes 8 | tf_op jit(solution)/shard_map/psum | solution.py:59
  218.3 2.5 collective-permute-start.5
  220.8 3.2 collective-permute-start.4
  224.2 1.8 collective-permute-done.5
  226.0 5.7 %collective-permute-done.4 = f32[1,256,256]{2,1,0:T(8,128)S(1)} collective-permute-done((f32[1,256,256]{2,1,0:T(8,128)S(1)}, f32[1,256,256]{2,1,0:T(8,128)S(1)}, u32[]{:S(2)}, u32[]{:S(2)}) %collective-permute-start.4) | collective-permute-done | bytes 262176 | tf_op jit(solution)/shard_map/ppermute | solution.py:18
  231.7 1.5 fusion.47
  233.2 89.6 %psum.38 = f32[]{:T(128)} all-reduce(f32[]{:T(128)} %fusion.47), channel_id=1, replica_groups=mesh['pos'=16,'slab'=32] {'slab'}, use_global_device_ids=true, to_apply=%region_7.8 | all-reduce | flops 1 | bytes 8 | tf_op jit(solution)/shard_map/psum | solution.py:72
  324.3 8.0 %collective-permute-start.7 = (f32[2,1,256,256]{3,2,1,0:T(8,128)S(1)}, f32[2,1,256,256]{3,2,1,0:T(8,128)S(1)}, u32[]{:S(2)}, u32[]{:S(2)}) collective-permute-start(f32[2,1,256,256]{3,2,1,0:T(8,128)S(1)} %get-tuple-element.10), channel_id=1, source_target_pairs={{0,1},{1,2},{2,3},{3,4},{4,5},{5,6},{6,7},{7,8},{8,9},{9,10},{10,1... | collective-permute-start | bytes 1572872 | tf_op jit(solution)/shard_map/ppermute | solution.py:17
  332.4 1.9 collective-permute-start.6
  335.3 5.6 %collective-permute-done.6 = f32[2,1,256,256]{3,2,1,0:T(8,128)S(1)} collective-permute-done((f32[2,1,256,256]{3,2,1,0:T(8,128)S(1)}, f32[2,1,256,256]{3,2,1,0:T(8,128)S(1)}, u32[]{:S(2)}, u32[]{:S(2)}) %collective-permute-start.6) | collective-permute-done | bytes 524320 | tf_op jit(solution)/shard_map/ppermute | solution.py:18
  341.4 0.8 copy-done.4
  342.4 4.0 fusion.14
  346.4 203.0 %all-reduce.7.cloned.1.call-done = f32[2,256,256]{2,1,0:T(8,128)} async-done(((f32[2,256,256]{2,1,0:T(8,128)}), f32[2,256,256]{2,1,0:T(8,128)}) %all-reduce.7.cloned.1.call-update) | async-done | bytes 524304 | tf_op jit(solution)/shard_map/psum | solution.py:81
  549.4 1.9 broadcast_multiply_fusion
  (39 shorter events, 3.6 us)
Async XLA Ops:
  7.2 3.8 copy-start.8
  7.2 4.5 copy-start.3
  7.2 542.2 %all-reduce.7.cloned.1.call-start = ((), (), s32[]{:S(2)}) async-start(), calls=%async_computation | async-start | bytes 1048576 | tf_op jit(solution)/shard_map/psum | solution.py:81
  8.3 18.1 %collective-permute-start.3 = (f32[1,256,256]{2,1,0:T(8,128)S(1)}, f32[1,256,256]{2,1,0:T(8,128)}, u32[]{:S(2)}, u32[]{:S(2)}) collective-permute-start(f32[1,256,256]{2,1,0:T(8,128)S(1)} %get-tuple-element.24), channel_id=1, source_target_pairs={{0,1},{1,2},{2,3},{3,4},{4,5},{5,6},{6,7},{7,8},{8,9},{9,10},{10,1... | collective-permute-start | bytes 786440 | tf_op jit(solution)/shard_map/ppermute | solution.py:17
  11.7 14.2 %copy-start = (f32[1,2,256,256]{3,2,1,0:T(8,128)S(1)}, f32[1,2,256,256]{3,2,1,0:T(8,128)}, u32[]{:S(2)}) copy-start(f32[1,2,256,256]{3,2,1,0:T(8,128)} %param.11) | copy-start | bytes 1572868
  14.7 11.7 %collective-permute-start.2 = (f32[1,256,256]{2,1,0:T(8,128)S(1)}, f32[1,256,256]{2,1,0:T(8,128)S(1)}, u32[]{:S(2)}, u32[]{:S(2)}) collective-permute-start(f32[1,256,256]{2,1,0:T(8,128)S(1)} %get-tuple-element.22), channel_id=1, source_target_pairs={{0,1},{1,2},{2,3},{3,4},{4,5},{5,6},{6,7},{7,8},{8,9},{9,10},{10,1... | collective-permute-start | bytes 786440 | tf_op jit(solution)/shard_map/ppermute | solution.py:17
  18.3 8.1 %collective-permute-start.1 = (f32[1,256,256]{2,1,0:T(8,128)S(1)}, f32[1,256,256]{2,1,0:T(8,128)S(1)}, u32[]{:S(2)}, u32[]{:S(2)}) collective-permute-start(f32[1,256,256]{2,1,0:T(8,128)S(1)} %get-tuple-element.23), channel_id=1, source_target_pairs={{1,0},{2,1},{3,2},{4,3},{5,4},{6,5},{7,6},{8,7},{9,8},{10,9},{11,1... | collective-permute-start | bytes 786440 | tf_op jit(solution)/shard_map/ppermute | solution.py:18
  20.3 9.5 %collective-permute-start = (f32[1,256,256]{2,1,0:T(8,128)S(1)}, f32[1,256,256]{2,1,0:T(8,128)S(1)}, u32[]{:S(2)}, u32[]{:S(2)}) collective-permute-start(f32[1,256,256]{2,1,0:T(8,128)S(1)} %get-tuple-element.21), channel_id=1, source_target_pairs={{1,0},{2,1},{3,2},{4,3},{5,4},{6,5},{7,6},{8,7},{9,8},{10,9},{11,1... | collective-permute-start | bytes 786440 | tf_op jit(solution)/shard_map/ppermute | solution.py:18
  29.7 2.6 copy-start.5
  218.3 7.7 %collective-permute-start.5 = (f32[1,256,256]{2,1,0:T(8,128)S(1)}, f32[1,256,256]{2,1,0:T(8,128)S(1)}, u32[]{:S(2)}, u32[]{:S(2)}) collective-permute-start(f32[1,256,256]{2,1,0:T(8,128)S(1)} %get-tuple-element.16), channel_id=1, source_target_pairs={{0,1},{1,2},{2,3},{3,4},{4,5},{5,6},{6,7},{7,8},{8,9},{9,10},{10,1... | collective-permute-start | bytes 786440 | tf_op jit(solution)/shard_map/ppermute | solution.py:17
  220.8 10.9 %copy-start.6 = (f32[1,256,256]{2,1,0:T(8,128)S(1)}, f32[1,256,256]{2,1,0:T(8,128)}, u32[]{:S(2)}) copy-start(f32[1,256,256]{2,1,0:T(8,128)} %copy-done.5) | copy-start | bytes 786436
  220.8 10.8 %collective-permute-start.4 = (f32[1,256,256]{2,1,0:T(8,128)S(1)}, f32[1,256,256]{2,1,0:T(8,128)S(1)}, u32[]{:S(2)}, u32[]{:S(2)}) collective-permute-start(f32[1,256,256]{2,1,0:T(8,128)S(1)} %get-tuple-element.15), channel_id=1, source_target_pairs={{1,0},{2,1},{3,2},{4,3},{5,4},{6,5},{7,6},{8,7},{9,8},{10,9},{11,1... | collective-permute-start | bytes 786440 | tf_op jit(solution)/shard_map/ppermute | solution.py:18
  233.2 91.1 %copy-start.2 = (f32[1,2,256,256]{3,2,1,0:T(8,128)S(1)}, f32[1,2,256,256]{3,2,1,0:T(8,128)}, u32[]{:S(2)}) copy-start(f32[1,2,256,256]{3,2,1,0:T(8,128)} %param.10) | copy-start | bytes 1572868
  324.2 16.7 %copy-start.1 = (f32[1,2,256,256]{3,2,1,0:T(8,128)}, f32[1,2,256,256]{3,2,1,0:T(8,128)S(1)}, u32[]{:S(2)}) copy-start(f32[1,2,256,256]{3,2,1,0:T(8,128)S(1)} %add_bitcast_fusion) | copy-start | bytes 1572868
  324.3 11.0 %collective-permute-start.7 = (f32[2,1,256,256]{3,2,1,0:T(8,128)S(1)}, f32[2,1,256,256]{3,2,1,0:T(8,128)S(1)}, u32[]{:S(2)}, u32[]{:S(2)}) collective-permute-start(f32[2,1,256,256]{3,2,1,0:T(8,128)S(1)} %get-tuple-element.10), channel_id=1, source_target_pairs={{0,1},{1,2},{2,3},{3,4},{4,5},{5,6},{6,7},{7,8},{8,9},{9,10},{10,1... | collective-permute-start | bytes 1572872 | tf_op jit(solution)/shard_map/ppermute | solution.py:17
  332.4 8.6 %collective-permute-start.6 = (f32[2,1,256,256]{3,2,1,0:T(8,128)S(1)}, f32[2,1,256,256]{3,2,1,0:T(8,128)S(1)}, u32[]{:S(2)}, u32[]{:S(2)}) collective-permute-start(f32[2,1,256,256]{3,2,1,0:T(8,128)S(1)} %get-tuple-element.9), channel_id=1, source_target_pairs={{1,0},{2,1},{3,2},{4,3},{5,4},{6,5},{7,6},{8,7},{9,8},{10,9},{11,1... | collective-permute-start | bytes 1572872 | tf_op jit(solution)/shard_map/ppermute | solution.py:18
  341.2 1.0 copy-start.4
  341.2 1.2 copy-start.7
Sparse Core Ops, SparseCore 0:
  346.5 202.8 all-reduce.6
where the time goes:
time: 559 us; the launch traced here: 558 us
  blocking collectives  272 us (49%)
  waiting for transfers between devices  219 us (39%)
  starting transfers between devices  28.7 us (5%)
  between operations  18.9 us (3%)
  other arithmetic  15.4 us (3%)
    psum x1, waiting for transfers between devices, local(): summed = lax.psum(contribution, 'pos')  203 us
    psum x2, blocking collectives, squares(): return lax.psum(jnp.sum(residual * residual), 'slab')  182 us
    psum x1, blocking collectives, local(): alpha = norm_now / lax.psum(jnp.sum(direction * image), 'slab')  89.6 us
    ppermute x4, starting transfers between devices, padded(): before = lax.ppermute(last, axis, up)  16.1 us
    ppermute x4, waiting for transfers between devices, padded(): after = lax.ppermute(first, axis, down)  14.6 us
    ppermute x4, starting transfers between devices, padded(): after = lax.ppermute(first, axis, down)  12.7 us
  transfers between devices with their start and end apart: 9, of which 5 were waited for; matrix products, arithmetic and copies ran while one was open for 1% of the time, Pallas kernels for 0%

commit v1 on v0

--- a/solution.py
+++ b/solution.py
@@ -78,7 +78,8 @@
     stacked = jnp.stack([potential[0], solution])
     padded_stack = padded(stacked, (("slab", 1),), 1)
     contribution = gradient_term(stacked, padded_stack, relief, magnet_mask)
-    summed = lax.psum(contribution, "pos")
+    parts = lax.all_gather(contribution, "pos", axis=0, tiled=False)
+    summed = parts.sum(axis=0)
     return (summed / lax.axis_size("pos"), solution[None])
 
 

time: 559 us -> 502 us (0.90)
  the two profiles are of different devices: /device:TPU:8 before, /device:TPU:1 now
where the time goes in v1:
time: 502 us; the launch traced here: 501 us
  blocking collectives  263 us (52%)
  waiting for transfers between devices  159 us (32%)
  starting transfers between devices  34 us (7%)
  other arithmetic  20.1 us (4%)
  between operations  18.9 us (4%)
  local copies, waits for them, and re-layouts  6.04 us (1%)
    psum x2, blocking collectives, squares(): return lax.psum(jnp.sum(residual * residual), 'slab')  175 us
    all_gather x1, waiting for transfers between devices, local(): parts = lax.all_gather(contribution, 'pos', axis=0, tiled=False)  151 us
    psum x1, blocking collectives, local(): alpha = norm_now / lax.psum(jnp.sum(direction * image), 'slab')  87.6 us
    ppermute x4, starting transfers between devices, padded(): after = lax.ppermute(first, axis, down)  25.1 us
  transfers between devices with their start and end apart: 9, of which 5 were waited for; matrix products, arithmetic and copies ran while one was open for 1% of the time, Pallas kernels for 0%

profile of v1, /device:TPU:1, one launch (start us, length us, event | category | flops | bytes accessed | tf_op | source)
XLA Modules:
  0.0 501.1 jit_solution(7463813606836417823)
XLA Ops:
  8.0 1.5 fusion.57
  9.4 4.5 select_add_fusion
  14.0 8.8 %collective-permute-start = (f32[1,256,256]{2,1,0:T(8,128)S(1)}, f32[1,256,256]{2,1,0:T(8,128)S(1)}, u32[]{:S(2)}, u32[]{:S(2)}) collective-permute-start(f32[1,256,256]{2,1,0:T(8,128)S(1)} %get-tuple-element.21), channel_id=1, source_target_pairs={{1,0},{2,1},{3,2},{4,3},{5,4},{6,5},{7,6},{8,7},{9,8},{10,9},{11,1... | collective-permute-start | bytes 786440 | tf_op jit(solution)/shard_map/ppermute | solution.py:18
  22.8 1.9 collective-permute-start.2
  24.7 1.1 slice_bitcast_fusion.1
  25.7 2.4 collective-permute-start.1
  28.2 3.1 collective-permute-start.3
  31.3 1.6 fusion.54
  32.9 1.2 fusion.53
  34.9 1.6 multiply_reduce_fusion.1
  36.5 89.0 %all-reduce.4 = (f32[]{:T(128)}, f32[]{:T(128)}) all-reduce(f32[]{:T(128)} %get-tuple-element.3, f32[]{:T(128)} %get-tuple-element.2), channel_id=1, replica_groups=mesh['pos'=16,'slab'=32] {'slab'}, use_global_device_ids=true, to_apply=%region_1.2 | all-reduce | flops 2 | bytes 16 | tf_op jit(solution)/shard_map/psum | solution.py:59
  127.5 86.4 %psum.30 = f32[]{:T(128)} all-reduce(f32[]{:T(128)} %multiply_reduce_fusion), channel_id=1, replica_groups=mesh['pos'=16,'slab'=32] {'slab'}, use_global_device_ids=true, to_apply=%region_5.6 | all-reduce | flops 1 | bytes 8 | tf_op jit(solution)/shard_map/psum | solution.py:59
  215.5 8.0 %collective-permute-start.4 = (f32[1,256,256]{2,1,0:T(8,128)S(1)}, f32[1,256,256]{2,1,0:T(8,128)S(1)}, u32[]{:S(2)}, u32[]{:S(2)}) collective-permute-start(f32[1,256,256]{2,1,0:T(8,128)S(1)} %get-tuple-element.15), channel_id=1, source_target_pairs={{1,0},{2,1},{3,2},{4,3},{5,4},{6,5},{7,6},{8,7},{9,8},{10,9},{11,1... | collective-permute-start | bytes 786440 | tf_op jit(solution)/shard_map/ppermute | solution.py:18
  223.5 1.9 collective-permute-start.5
  225.6 3.1 collective-permute-done.5
  228.7 2.6 fusion.47
  231.3 87.6 %psum.31 = f32[]{:T(128)} all-reduce(f32[]{:T(128)} %fusion.47), channel_id=1, replica_groups=mesh['pos'=16,'slab'=32] {'slab'}, use_global_device_ids=true, to_apply=%region_7.8 | all-reduce | flops 1 | bytes 8 | tf_op jit(solution)/shard_map/psum | solution.py:72
  320.5 5.9 %collective-permute-start.6 = (f32[2,1,256,256]{3,2,1,0:T(8,128)S(1)}, f32[2,1,256,256]{3,2,1,0:T(8,128)S(1)}, u32[]{:S(2)}, u32[]{:S(2)}) collective-permute-start(f32[2,1,256,256]{3,2,1,0:T(8,128)S(1)} %get-tuple-element.9), channel_id=1, source_target_pairs={{1,0},{2,1},{3,2},{4,3},{5,4},{6,5},{7,6},{8,7},{9,8},{10,9},{11,1... | collective-permute-start | bytes 1572872 | tf_op jit(solution)/shard_map/ppermute | solution.py:18
  326.4 1.9 collective-permute-start.7
  329.3 1.8 collective-permute-done.6
  331.1 3.3 collective-permute-done.7
  334.9 4.0 fusion.14
  338.9 150.5 %all-gather.3.cloned.1.call-done = f32[32,256,256]{2,1,0:T(8,128)} async-done(((f32[2,256,256]{2,1,0:T(8,128)}), f32[32,256,256]{2,1,0:T(8,128)}) %all-gather.3.cloned.1.call-update) | async-done | bytes 8388624 | tf_op jit(solution)/shard_map/all_gather | solution.py:81
  489.5 4.0 reduce_sum.49
  (38 shorter events, 4.5 us)
Async XLA Ops:
  7.2 27.7 %copy-start = (f32[1,2,256,256]{3,2,1,0:T(8,128)S(1)}, f32[1,2,256,256]{3,2,1,0:T(8,128)}, u32[]{:S(2)}) copy-start(f32[1,2,256,256]{3,2,1,0:T(8,128)} %param.11) | copy-start | bytes 1572868
  7.2 482.3 %all-gather.3.cloned.1.call-start = ((), (), s32[]{:S(2)}) async-start(), calls=%async_computation | async-start | bytes 8912896 | tf_op jit(solution)/shard_map/all_gather | solution.py:81
  14.0 20.2 %collective-permute-start = (f32[1,256,256]{2,1,0:T(8,128)S(1)}, f32[1,256,256]{2,1,0:T(8,128)S(1)}, u32[]{:S(2)}, u32[]{:S(2)}) collective-permute-start(f32[1,256,256]{2,1,0:T(8,128)S(1)} %get-tuple-element.21), channel_id=1, source_target_pairs={{1,0},{2,1},{3,2},{4,3},{5,4},{6,5},{7,6},{8,7},{9,8},{10,9},{11,1... | collective-permute-start | bytes 786440 | tf_op jit(solution)/shard_map/ppermute | solution.py:18
  22.8 11.4 %collective-permute-start.2 = (f32[1,256,256]{2,1,0:T(8,128)S(1)}, f32[1,256,256]{2,1,0:T(8,128)S(1)}, u32[]{:S(2)}, u32[]{:S(2)}) collective-permute-start(f32[1,256,256]{2,1,0:T(8,128)S(1)} %get-tuple-element.22), channel_id=1, source_target_pairs={{0,1},{1,2},{2,3},{3,4},{4,5},{5,6},{6,7},{7,8},{8,9},{9,10},{10,1... | collective-permute-start | bytes 786440 | tf_op jit(solution)/shard_map/ppermute | solution.py:17
  25.7 8.5 %collective-permute-start.1 = (f32[1,256,256]{2,1,0:T(8,128)S(1)}, f32[1,256,256]{2,1,0:T(8,128)S(1)}, u32[]{:S(2)}, u32[]{:S(2)}) collective-permute-start(f32[1,256,256]{2,1,0:T(8,128)S(1)} %get-tuple-element.23), channel_id=1, source_target_pairs={{1,0},{2,1},{3,2},{4,3},{5,4},{6,5},{7,6},{8,7},{9,8},{10,9},{11,1... | collective-permute-start | bytes 786440 | tf_op jit(solution)/shard_map/ppermute | solution.py:18
  28.2 6.4 %collective-permute-start.3 = (f32[1,256,256]{2,1,0:T(8,128)S(1)}, f32[1,256,256]{2,1,0:T(8,128)S(1)}, u32[]{:S(2)}, u32[]{:S(2)}) collective-permute-start(f32[1,256,256]{2,1,0:T(8,128)S(1)} %get-tuple-element.24), channel_id=1, source_target_pairs={{0,1},{1,2},{2,3},{3,4},{4,5},{5,6},{6,7},{7,8},{8,9},{9,10},{10,1... | collective-permute-start | bytes 786440 | tf_op jit(solution)/shard_map/ppermute | solution.py:17
  34.1 0.7 copy-start.3
  34.2 2.3 copy-start.5
  34.2 2.3 copy-start.6
  36.5 283.9 %copy-start.2 = (f32[1,2,256,256]{3,2,1,0:T(8,128)S(1)}, f32[1,2,256,256]{3,2,1,0:T(8,128)}, u32[]{:S(2)}) copy-start(f32[1,2,256,256]{3,2,1,0:T(8,128)} %param.10) | copy-start | bytes 1572868
  215.5 10.2 %collective-permute-start.4 = (f32[1,256,256]{2,1,0:T(8,128)S(1)}, f32[1,256,256]{2,1,0:T(8,128)S(1)}, u32[]{:S(2)}, u32[]{:S(2)}) collective-permute-start(f32[1,256,256]{2,1,0:T(8,128)S(1)} %get-tuple-element.15), channel_id=1, source_target_pairs={{1,0},{2,1},{3,2},{4,3},{5,4},{6,5},{7,6},{8,7},{9,8},{10,9},{11,1... | collective-permute-start | bytes 786440 | tf_op jit(solution)/shard_map/ppermute | solution.py:18
  223.5 5.2 %collective-permute-start.5 = (f32[1,256,256]{2,1,0:T(8,128)S(1)}, f32[1,256,256]{2,1,0:T(8,128)S(1)}, u32[]{:S(2)}, u32[]{:S(2)}) collective-permute-start(f32[1,256,256]{2,1,0:T(8,128)S(1)} %get-tuple-element.16), channel_id=1, source_target_pairs={{0,1},{1,2},{2,3},{3,4},{4,5},{5,6},{6,7},{7,8},{8,9},{9,10},{10,1... | collective-permute-start | bytes 786440 | tf_op jit(solution)/shard_map/ppermute | solution.py:17
  320.4 14.5 %copy-start.1 = (f32[1,2,256,256]{3,2,1,0:T(8,128)}, f32[1,2,256,256]{3,2,1,0:T(8,128)S(1)}, u32[]{:S(2)}) copy-start(f32[1,2,256,256]{3,2,1,0:T(8,128)S(1)} %add_bitcast_fusion) | copy-start | bytes 1572868
  320.5 14.4 %copy-start.4 = (s32[2,256,256]{2,1,0:T(8,128)S(1)}, s32[2,256,256]{2,1,0:T(8,128)}, u32[]{:S(2)}) copy-start(s32[2,256,256]{2,1,0:T(8,128)} %param.6) | copy-start | bytes 1572868
  320.5 14.4 %copy-start.7 = (s32[2,256,256]{2,1,0:T(8,128)S(1)}, s32[2,256,256]{2,1,0:T(8,128)}, u32[]{:S(2)}) copy-start(s32[2,256,256]{2,1,0:T(8,128)} %param.7) | copy-start | bytes 1572868
  320.5 10.6 %collective-permute-start.6 = (f32[2,1,256,256]{3,2,1,0:T(8,128)S(1)}, f32[2,1,256,256]{3,2,1,0:T(8,128)S(1)}, u32[]{:S(2)}, u32[]{:S(2)}) collective-permute-start(f32[2,1,256,256]{3,2,1,0:T(8,128)S(1)} %get-tuple-element.9), channel_id=1, source_target_pairs={{1,0},{2,1},{3,2},{4,3},{5,4},{6,5},{7,6},{8,7},{9,8},{10,9},{11,1... | collective-permute-start | bytes 1572872 | tf_op jit(solution)/shard_map/ppermute | solution.py:18
  326.4 8.0 %collective-permute-start.7 = (f32[2,1,256,256]{3,2,1,0:T(8,128)S(1)}, f32[2,1,256,256]{3,2,1,0:T(8,128)S(1)}, u32[]{:S(2)}, u32[]{:S(2)}) collective-permute-start(f32[2,1,256,256]{3,2,1,0:T(8,128)S(1)} %get-tuple-element.10), channel_id=1, source_target_pairs={{0,1},{1,2},{2,3},{3,4},{4,5},{5,6},{6,7},{7,8},{8,9},{9,10},{10,1... | collective-permute-start | bytes 1572872 | tf_op jit(solution)/shard_map/ppermute | solution.py:17
Sparse Core Ops, SparseCore 0:
  339.1 150.3 all-gather.2
